TPU v7x, 512 devices: a whole 4x8x8 slice. The times are simulated.
512 devices in a mesh: layer: 32 (over x_lo, y, core), feat: 16 (over z, x_hi).
Axes of the slice: x: 4 (x_hi: 2, x_lo: 2; x = x_hi * 2 + x_lo), y: 8, z: 8, core: 2. Of those that a mesh axis runs over, the one named last changes fastest.
Arguments:
- latents: bfloat16 [2048, 16384], P('layer', 'feat'), may hold values from 0.5 to 3
- block_lists: int32 [4, 16, 64], replicated, may hold values from 0 to 127, all different within a row
- decoders: bfloat16 [2, 16384, 32768], P(None, 'feat', 'layer'), may hold values from -0.03125 to 0.03125
- targets: bfloat16 [512, 32768], P('feat', 'layer'), may hold values from -6 to 6
Outputs:
- errors: bfloat16 [512, 32768], P('feat', 'layer')
- latent_grad: float32 [2048, 16384], P('layer', 'feat')
Inputs may be any that keep to these rules, and one draw needn't show every extreme that they name: `block_lists`: each row names 64 different latent blocks, and every block is named by some row.
All inputs are finite; a program needn't handle non-finite values.
Results may differ from a plain program's by a relative error of at most 0.006.
Values may be sent and summed in bfloat16 or wider, within the bound.
No kernel may reach another device: no remote copies, remote signals or barrier semaphores. Data moves between devices by JAX's collectives and lax.ppermute only.
A program may use at most 64 MiB of HBM per device.

v0:
```python
import jax
import jax.numpy as jnp
from jax import lax
from jax.sharding import PartitionSpec as P


D = 8192
BLOCK = 128
TROWS = 32
CORES = 2


def swap_cores(value):
    count = lax.axis_size("layer")
    return lax.ppermute(value, "layer", [(source, source ^ 1) for source in range(count)])


def mirrored(value, groups, steps):
    count = lax.axis_size("layer")
    chips = groups // CORES
    pairs = []
    for source in range(count):
        start = source // groups * groups + steps
        chip, core = source % groups // CORES, source % CORES
        if 0 <= start < count:
            pairs.append((source, start + (chips - 1 - chip) * CORES + core))
    return lax.ppermute(value, "layer", pairs)


def to_chip(value, turn):
    count = lax.axis_size("layer")
    return lax.ppermute(
        value, "layer", [(source, source ^ (turn * CORES)) for source in range(count)]
    )


def ordered(upper, held, partner, axis):
    return jnp.stack(
        [jnp.where(upper, partner, held), jnp.where(upper, held, partner)], axis
    )


def halves(upper, value, axis):
    lower = lax.index_in_dim(value, 0, axis, keepdims=False)
    higher = lax.index_in_dim(value, 1, axis, keepdims=False)
    return jnp.where(upper, higher, lower), jnp.where(upper, lower, higher)


def over_feat(value):
    return lax.all_to_all(value, "feat", 0, 0, tiled=True)


def local(latents, block_lists, decoders, targets):
    layer_pos = lax.axis_index("layer")
    feat_pos = lax.axis_index("feat")
    feats = lax.axis_size("feat")
    width_cols = decoders.shape[2]
    groups = D // width_cols
    chips = groups // CORES
    layer_id = layer_pos // groups
    member = layer_pos % groups
    upper_core = member % CORES == 1
    upper_chip = member // CORES % 2 == 1
    upper_pair = member // (2 * CORES) % 2 == 1
    rows_here, feat_cols = latents.shape
    total_rows = rows_here * groups
    blocks_here = feat_cols // BLOCK
    lists_here = rows_here // TROWS

    lists = lax.dynamic_slice(
        block_lists,
        (layer_id, member * lists_here, 0),
        (1, lists_here, block_lists.shape[2]),
    )[0]
    wanted = feat_pos * blocks_here + jnp.arange(blocks_here, dtype=jnp.int32)
    hit = jnp.any(lists[:, :, None] == wanted[None, None, :], axis=1)
    tile_mask = jnp.repeat(jnp.repeat(hit, TROWS, axis=0), BLOCK, axis=1)
    own_tile = jnp.where(tile_mask, latents, jnp.zeros_like(latents))
    prior_tile = mirrored(own_tile, groups, groups)

    def spread_over_chips(piece, high, low):
        far = to_chip(piece, 2)
        pair = ordered(high, piece, far, 0)
        near = to_chip(pair, 1)
        return ordered(low, pair, near, 1).reshape(chips, rows_here, feat_cols)

    own_mine = spread_over_chips(own_tile, upper_pair, upper_chip)
    prior_mine = spread_over_chips(
        prior_tile, jnp.logical_not(upper_pair), jnp.logical_not(upper_chip)
    )
    own_theirs = swap_cores(own_mine)
    prior_theirs = swap_cores(prior_mine)
    acts_own = ordered(upper_core, own_mine, own_theirs, 1)
    own_part = jnp.dot(
        acts_own.reshape(total_rows, feat_cols),
        decoders[0],
        preferred_element_type=jnp.float32,
    )
    acts_prior = ordered(lax.optimization_barrier(upper_core), prior_mine, prior_theirs, 1)
    prior_part = jnp.dot(
        acts_prior.reshape(total_rows, feat_cols),
        decoders[1],
        preferred_element_type=jnp.float32,
    )
    summed = prior_part + own_part
    parts = over_feat(summed.astype(jnp.bfloat16).reshape(feats, -1, width_cols))
    recon = jnp.sum(parts.astype(jnp.float32), axis=0)
    errors = (recon - targets.astype(jnp.float32)).astype(jnp.bfloat16)
    spread = over_feat(jnp.broadcast_to(errors[None], (feats,) + errors.shape))
    spread = spread.reshape(total_rows, width_cols)

    def paired(weights):
        terms = jnp.einsum("tc,fc->tf", spread, weights, preferred_element_type=jnp.float32)
        terms = terms.reshape(chips, CORES, rows_here, feat_cols)
        kept, sent = halves(upper_core, terms, 1)
        return kept + swap_cores(sent.astype(jnp.bfloat16)).astype(jnp.float32)

    def summed_over_chips(total, high, low):
        total = total.reshape(2, chips // 2, rows_here, feat_cols)
        kept, sent = halves(low, total, 1)
        near = to_chip(sent.astype(jnp.bfloat16), 1)
        total = kept + near.astype(jnp.float32)
        kept, sent = halves(high, total, 0)
        far = to_chip(sent.astype(jnp.bfloat16), 2)
        return kept + far.astype(jnp.float32)

    to_prior = summed_over_chips(
        paired(decoders[1]), jnp.logical_not(upper_pair), jnp.logical_not(upper_chip)
    )
    from_next = mirrored(to_prior.astype(jnp.bfloat16), groups, -groups)
    from_next = from_next.astype(jnp.float32)
    combined = summed_over_chips(paired(decoders[0]), upper_pair, upper_chip) + from_next
    latent_grad = jnp.where(tile_mask, combined, jnp.zeros_like(combined))
    return (errors, latent_grad)


def solution(mesh):
    placed = (P("layer", "feat"), P(), P(None, "feat", "layer"), P("feat", "layer"))
    return jax.shard_map(
        local,
        mesh=mesh,
        in_specs=placed,
        out_specs=(P("feat", "layer"), P("layer", "feat")),
        check_vma=False,
    )
```

profile of v0, /device:TPU:2, one launch (start us, length us, event | category | flops | bytes accessed | tf_op | source)
XLA Modules:
  0.0 159.4 jit_solution(9028870812034317982)
XLA Ops:
  1.7 0.9 bitcast_select_fusion.1
  2.7 5.4 %collective-permute-start = (bf16[64,1024]{1,0:T(8,128)(2,1)S(1)}, bf16[64,1024]{1,0:T(8,128)(2,1)S(1)}, u32[]{:S(2)}, u32[]{:S(2)}) collective-permute-start(bf16[64,1024]{1,0:T(8,128)(2,1)S(1)} %bitcast_select_fusion.1), channel_id=1, source_target_pairs={{0,224},{16,240},{32,192},{48,208},{64,160},{80,176},{96,128},{112... | collective-permute-start | bytes 393224 | tf_op jit(solution)/shard_map/ppermute | solution.py:27
  8.1 4.9 %collective-permute-start.4 = (bf16[64,1024]{1,0:T(8,128)(2,1)S(1)}, bf16[64,1024]{1,0:T(8,128)(2,1)S(1)}, u32[]{:S(2)}, u32[]{:S(2)}) collective-permute-start(bf16[64,1024]{1,0:T(8,128)(2,1)S(1)} %bitcast_select_fusion.1), channel_id=1, source_target_pairs={{0,64},{16,80},{32,96},{48,112},{64,0},{80,16},{96,32},{112,48},{1... | collective-permute-start | bytes 393224 | tf_op jit(solution)/shard_map/ppermute | solution.py:32
  13.1 1.6 %collective-permute-done = bf16[64,1024]{1,0:T(8,128)(2,1)S(1)} collective-permute-done((bf16[64,1024]{1,0:T(8,128)(2,1)S(1)}, bf16[64,1024]{1,0:T(8,128)(2,1)S(1)}, u32[]{:S(2)}, u32[]{:S(2)}) %collective-permute-start) | collective-permute-done | bytes 131104 | tf_op jit(solution)/shard_map/ppermute | solution.py:27
  14.7 3.7 %collective-permute-start.1 = (bf16[64,1024]{1,0:T(8,128)(2,1)S(1)}, bf16[64,1024]{1,0:T(8,128)(2,1)S(1)}, u32[]{:S(2)}, u32[]{:S(2)}) collective-permute-start(bf16[64,1024]{1,0:T(8,128)(2,1)S(1)} %collective-permute-done), channel_id=1, source_target_pairs={{0,64},{16,80},{32,96},{48,112},{64,0},{80,16},{96,32},{112,48},{1... | collective-permute-start | bytes 393224 | tf_op jit(solution)/shard_map/ppermute | solution.py:32
  18.4 1.6 %collective-permute-done.4 = bf16[64,1024]{1,0:T(8,128)(2,1)S(1)} collective-permute-done((bf16[64,1024]{1,0:T(8,128)(2,1)S(1)}, bf16[64,1024]{1,0:T(8,128)(2,1)S(1)}, u32[]{:S(2)}, u32[]{:S(2)}) %collective-permute-start.4) | collective-permute-done | bytes 131104 | tf_op jit(solution)/shard_map/ppermute | solution.py:32
  20.1 2.7 %collective-permute-start.5 = (bf16[2,64,1024]{2,1,0:T(8,128)(2,1)S(1)}, bf16[2,64,1024]{2,1,0:T(8,128)(2,1)S(1)}, u32[]{:S(2)}, u32[]{:S(2)}) collective-permute-start(bf16[2,64,1024]{2,1,0:T(8,128)(2,1)S(1)} %pad_maximum_fusion.5), channel_id=1, source_target_pairs={{0,32},{16,48},{32,0},{48,16},{64,96},{80,112},{96,64},{112,80},{1... | collective-permute-start | bytes 786440 | tf_op jit(solution)/shard_map/ppermute | solution.py:32
  22.8 2.0 %collective-permute-done.1 = bf16[64,1024]{1,0:T(8,128)(2,1)S(1)} collective-permute-done((bf16[64,1024]{1,0:T(8,128)(2,1)S(1)}, bf16[64,1024]{1,0:T(8,128)(2,1)S(1)}, u32[]{:S(2)}, u32[]{:S(2)}) %collective-permute-start.1) | collective-permute-done | bytes 131104 | tf_op jit(solution)/shard_map/ppermute | solution.py:32
  24.9 1.9 %collective-permute-start.2 = (bf16[2,64,1024]{2,1,0:T(8,128)(2,1)S(1)}, bf16[2,64,1024]{2,1,0:T(8,128)(2,1)S(1)}, u32[]{:S(2)}, u32[]{:S(2)}) collective-permute-start(bf16[2,64,1024]{2,1,0:T(8,128)(2,1)S(1)} %pad_maximum_fusion.4), channel_id=1, source_target_pairs={{0,32},{16,48},{32,0},{48,16},{64,96},{80,112},{96,64},{112,80},{1... | collective-permute-start | bytes 786440 | tf_op jit(solution)/shard_map/ppermute | solution.py:32
  26.8 4.4 %collective-permute-done.5 = bf16[2,64,1024]{2,1,0:T(8,128)(2,1)S(1)} collective-permute-done((bf16[2,64,1024]{2,1,0:T(8,128)(2,1)S(1)}, bf16[2,64,1024]{2,1,0:T(8,128)(2,1)S(1)}, u32[]{:S(2)}, u32[]{:S(2)}) %collective-permute-start.5) | collective-permute-done | bytes 262176 | tf_op jit(solution)/shard_map/ppermute | solution.py:32
  31.3 1.9 %collective-permute-start.6 = (bf16[4,64,1024]{2,1,0:T(8,128)(2,1)S(1)}, bf16[4,64,1024]{2,1,0:T(8,128)(2,1)S(1)}, u32[]{:S(2)}, u32[]{:S(2)}) collective-permute-start(bf16[4,64,1024]{2,1,0:T(8,128)(2,1)S(1)} %bitcast.148), channel_id=1, source_target_pairs={{0,16},{16,0},{32,48},{48,32},{64,80},{80,64},{96,112},{112,96},{1... | collective-permute-start | bytes 1572872 | tf_op jit(solution)/shard_map/ppermute | solution.py:15
  33.2 2.1 %collective-permute-done.2 = bf16[2,64,1024]{2,1,0:T(8,128)(2,1)S(1)} collective-permute-done((bf16[2,64,1024]{2,1,0:T(8,128)(2,1)S(1)}, bf16[2,64,1024]{2,1,0:T(8,128)(2,1)S(1)}, u32[]{:S(2)}, u32[]{:S(2)}) %collective-permute-start.2) | collective-permute-done | bytes 262176 | tf_op jit(solution)/shard_map/ppermute | solution.py:32
  35.5 1.9 %collective-permute-start.3 = (bf16[4,64,1024]{2,1,0:T(8,128)(2,1)S(1)}, bf16[4,64,1024]{2,1,0:T(8,128)(2,1)S(1)}, u32[]{:S(2)}, u32[]{:S(2)}) collective-permute-start(bf16[4,64,1024]{2,1,0:T(8,128)(2,1)S(1)} %bitcast.149), channel_id=1, source_target_pairs={{0,16},{16,0},{32,48},{48,32},{64,80},{80,64},{96,112},{112,96},{1... | collective-permute-start | bytes 1572872 | tf_op jit(solution)/shard_map/ppermute | solution.py:15
  37.7 2.0 %copy-done.3 = bf16[2,1024,1024]{2,1,0:T(8,128)(2,1)S(1)} copy-done((bf16[2,1024,1024]{2,1,0:T(8,128)(2,1)S(1)}, bf16[2,1024,1024]{2,1,0:T(8,128)(2,1)}, u32[]{:S(2)}) %copy-start.3) | copy-done | bytes 4194328
  39.7 1.3 fusion.4
  41.3 1.3 add_convert_fusion
  42.6 43.2 %all_to_all.10 = bf16[16,32,1024]{2,1,0:T(8,128)(2,1)S(1)} all-to-all(bf16[16,32,1024]{2,1,0:T(8,128)(2,1)S(1)} %bitcast.153), channel_id=1, replica_groups=mesh['layer'=32,'feat'=16] {'feat'}, dimensions={0} | all-to-all | bytes 2097152 | tf_op jit(solution)/shard_map/all_to_all | solution.py:50
  86.1 32.2 %all_to_all.11 = bf16[16,32,1024]{2,1,0:T(8,128)(2,1)S(1)} all-to-all(bf16[16,32,1024]{2,1,0:T(8,128)(2,1)S(1)} %broadcast_in_dim.22), channel_id=1, replica_groups=mesh['layer'=32,'feat'=16] {'feat'}, dimensions={0} | all-to-all | bytes 2097152 | tf_op jit(solution)/shard_map/all_to_all | solution.py:50
  118.3 1.3 fusion
  119.7 1.9 %collective-permute-start.10 = (bf16[4,64,1024]{2,1,0:T(8,128)(2,1)S(1)}, bf16[4,64,1024]{2,1,0:T(8,128)(2,1)S(1)}, u32[]{:S(2)}, u32[]{:S(2)}) collective-permute-start(bf16[4,64,1024]{2,1,0:T(8,128)(2,1)S(1)} %fusion.18), channel_id=1, source_target_pairs={{0,16},{16,0},{32,48},{48,32},{64,80},{80,64},{96,112},{112,96},{1... | collective-permute-start | bytes 1572872 | tf_op jit(solution)/shard_map/ppermute | solution.py:15
  121.7 1.3 fusion.2
  123.0 2.4 %collective-permute-start.7 = (bf16[4,64,1024]{2,1,0:T(8,128)(2,1)S(1)}, bf16[4,64,1024]{2,1,0:T(8,128)(2,1)S(1)}, u32[]{:S(2)}, u32[]{:S(2)}) collective-permute-start(bf16[4,64,1024]{2,1,0:T(8,128)(2,1)S(1)} %fusion.17), channel_id=1, source_target_pairs={{0,16},{16,0},{32,48},{48,32},{64,80},{80,64},{96,112},{112,96},{1... | collective-permute-start | bytes 1572872 | tf_op jit(solution)/shard_map/ppermute | solution.py:15
  125.8 2.1 %collective-permute-start.11 = (bf16[2,64,1024]{2,1,0:T(8,128)(2,1)S(1)}, bf16[2,64,1024]{2,1,0:T(8,128)(2,1)S(1)}, u32[]{:S(2)}, u32[]{:S(2)}) collective-permute-start(bf16[2,64,1024]{2,1,0:T(8,128)(2,1)S(1)} %fusion.20), channel_id=1, source_target_pairs={{0,32},{16,48},{32,0},{48,16},{64,96},{80,112},{96,64},{112,80},{1... | collective-permute-start | bytes 786440 | tf_op jit(solution)/shard_map/ppermute | solution.py:32
  128.2 3.7 %collective-permute-start.8 = (bf16[2,64,1024]{2,1,0:T(8,128)(2,1)S(1)}, bf16[2,64,1024]{2,1,0:T(8,128)(2,1)S(1)}, u32[]{:S(2)}, u32[]{:S(2)}) collective-permute-start(bf16[2,64,1024]{2,1,0:T(8,128)(2,1)S(1)} %fusion.19), channel_id=1, source_target_pairs={{0,32},{16,48},{32,0},{48,16},{64,96},{80,112},{96,64},{112,80},{1... | collective-permute-start | bytes 786440 | tf_op jit(solution)/shard_map/ppermute | solution.py:32
  132.0 4.9 %collective-permute-done.11 = bf16[2,64,1024]{2,1,0:T(8,128)(2,1)S(1)} collective-permute-done((bf16[2,64,1024]{2,1,0:T(8,128)(2,1)S(1)}, bf16[2,64,1024]{2,1,0:T(8,128)(2,1)S(1)}, u32[]{:S(2)}, u32[]{:S(2)}) %collective-permute-start.11) | collective-permute-done | bytes 262176 | tf_op jit(solution)/shard_map/ppermute | solution.py:32
  137.0 3.5 %collective-permute-start.12 = (bf16[64,1024]{1,0:T(8,128)(2,1)S(1)}, bf16[64,1024]{1,0:T(8,128)(2,1)S(1)}, u32[]{:S(2)}, u32[]{:S(2)}) collective-permute-start(bf16[64,1024]{1,0:T(8,128)(2,1)S(1)} %fusion.25), channel_id=1, source_target_pairs={{0,64},{16,80},{32,96},{48,112},{64,0},{80,16},{96,32},{112,48},{1... | collective-permute-start | bytes 393224 | tf_op jit(solution)/shard_map/ppermute | solution.py:32
  140.5 2.5 %collective-permute-done.8 = bf16[2,64,1024]{2,1,0:T(8,128)(2,1)S(1)} collective-permute-done((bf16[2,64,1024]{2,1,0:T(8,128)(2,1)S(1)}, bf16[2,64,1024]{2,1,0:T(8,128)(2,1)S(1)}, u32[]{:S(2)}, u32[]{:S(2)}) %collective-permute-start.8) | collective-permute-done | bytes 262176 | tf_op jit(solution)/shard_map/ppermute | solution.py:32
  143.1 3.0 %collective-permute-start.9 = (bf16[64,1024]{1,0:T(8,128)(2,1)S(1)}, bf16[64,1024]{1,0:T(8,128)(2,1)S(1)}, u32[]{:S(2)}, u32[]{:S(2)}) collective-permute-start(bf16[64,1024]{1,0:T(8,128)(2,1)S(1)} %fusion.24), channel_id=1, source_target_pairs={{0,64},{16,80},{32,96},{48,112},{64,0},{80,16},{96,32},{112,48},{1... | collective-permute-start | bytes 393224 | tf_op jit(solution)/shard_map/ppermute | solution.py:32
  146.1 4.4 %collective-permute-done.12 = bf16[64,1024]{1,0:T(8,128)(2,1)S(1)} collective-permute-done((bf16[64,1024]{1,0:T(8,128)(2,1)S(1)}, bf16[64,1024]{1,0:T(8,128)(2,1)S(1)}, u32[]{:S(2)}, u32[]{:S(2)}) %collective-permute-start.12) | collective-permute-done | bytes 131104 | tf_op jit(solution)/shard_map/ppermute | solution.py:32
  150.5 3.9 %collective-permute-start.13 = (bf16[64,1024]{1,0:T(8,128)(2,1)S(1)}, bf16[64,1024]{1,0:T(8,128)(2,1)S(1)}, u32[]{:S(2)}, u32[]{:S(2)}) collective-permute-start(bf16[64,1024]{1,0:T(8,128)(2,1)S(1)} %fusion.21), channel_id=1, source_target_pairs={{128,96},{144,112},{160,64},{176,80},{192,32},{208,48},{224,0},{24... | collective-permute-start | bytes 393224 | tf_op jit(solution)/shard_map/ppermute | solution.py:27
  154.5 4.1 %collective-permute-done.13 = bf16[64,1024]{1,0:T(8,128)(2,1)S(1)} collective-permute-done((bf16[64,1024]{1,0:T(8,128)(2,1)S(1)}, bf16[64,1024]{1,0:T(8,128)(2,1)S(1)}, u32[]{:S(2)}, u32[]{:S(2)}) %collective-permute-start.13) | collective-permute-done | bytes 131104 | tf_op jit(solution)/shard_map/ppermute | solution.py:27
  158.6 0.8 fusion.23
  (46 shorter events, 3.4 us)
Async XLA Ops:
  0.6 0.8 copy-start
  2.7 12.0 %collective-permute-start = (bf16[64,1024]{1,0:T(8,128)(2,1)S(1)}, bf16[64,1024]{1,0:T(8,128)(2,1)S(1)}, u32[]{:S(2)}, u32[]{:S(2)}) collective-permute-start(bf16[64,1024]{1,0:T(8,128)(2,1)S(1)} %bitcast_select_fusion.1), channel_id=1, source_target_pairs={{0,224},{16,240},{32,192},{48,208},{64,160},{80,176},{96,128},{112... | collective-permute-start | bytes 393224 | tf_op jit(solution)/shard_map/ppermute | solution.py:27
  8.1 11.9 %collective-permute-start.4 = (bf16[64,1024]{1,0:T(8,128)(2,1)S(1)}, bf16[64,1024]{1,0:T(8,128)(2,1)S(1)}, u32[]{:S(2)}, u32[]{:S(2)}) collective-permute-start(bf16[64,1024]{1,0:T(8,128)(2,1)S(1)} %bitcast_select_fusion.1), channel_id=1, source_target_pairs={{0,64},{16,80},{32,96},{48,112},{64,0},{80,16},{96,32},{112,48},{1... | collective-permute-start | bytes 393224 | tf_op jit(solution)/shard_map/ppermute | solution.py:32
  14.7 10.1 %collective-permute-start.1 = (bf16[64,1024]{1,0:T(8,128)(2,1)S(1)}, bf16[64,1024]{1,0:T(8,128)(2,1)S(1)}, u32[]{:S(2)}, u32[]{:S(2)}) collective-permute-start(bf16[64,1024]{1,0:T(8,128)(2,1)S(1)} %collective-permute-done), channel_id=1, source_target_pairs={{0,64},{16,80},{32,96},{48,112},{64,0},{80,16},{96,32},{112,48},{1... | collective-permute-start | bytes 393224 | tf_op jit(solution)/shard_map/ppermute | solution.py:32
  20.1 11.1 %collective-permute-start.5 = (bf16[2,64,1024]{2,1,0:T(8,128)(2,1)S(1)}, bf16[2,64,1024]{2,1,0:T(8,128)(2,1)S(1)}, u32[]{:S(2)}, u32[]{:S(2)}) collective-permute-start(bf16[2,64,1024]{2,1,0:T(8,128)(2,1)S(1)} %pad_maximum_fusion.5), channel_id=1, source_target_pairs={{0,32},{16,48},{32,0},{48,16},{64,96},{80,112},{96,64},{112,80},{1... | collective-permute-start | bytes 786440 | tf_op jit(solution)/shard_map/ppermute | solution.py:32
  24.9 10.5 %collective-permute-start.2 = (bf16[2,64,1024]{2,1,0:T(8,128)(2,1)S(1)}, bf16[2,64,1024]{2,1,0:T(8,128)(2,1)S(1)}, u32[]{:S(2)}, u32[]{:S(2)}) collective-permute-start(bf16[2,64,1024]{2,1,0:T(8,128)(2,1)S(1)} %pad_maximum_fusion.4), channel_id=1, source_target_pairs={{0,32},{16,48},{32,0},{48,16},{64,96},{80,112},{96,64},{112,80},{1... | collective-permute-start | bytes 786440 | tf_op jit(solution)/shard_map/ppermute | solution.py:32
  31.3 6.1 %collective-permute-start.6 = (bf16[4,64,1024]{2,1,0:T(8,128)(2,1)S(1)}, bf16[4,64,1024]{2,1,0:T(8,128)(2,1)S(1)}, u32[]{:S(2)}, u32[]{:S(2)}) collective-permute-start(bf16[4,64,1024]{2,1,0:T(8,128)(2,1)S(1)} %bitcast.148), channel_id=1, source_target_pairs={{0,16},{16,0},{32,48},{48,32},{64,80},{80,64},{96,112},{112,96},{1... | collective-permute-start | bytes 1572872 | tf_op jit(solution)/shard_map/ppermute | solution.py:15
  35.5 5.5 %collective-permute-start.3 = (bf16[4,64,1024]{2,1,0:T(8,128)(2,1)S(1)}, bf16[4,64,1024]{2,1,0:T(8,128)(2,1)S(1)}, u32[]{:S(2)}, u32[]{:S(2)}) collective-permute-start(bf16[4,64,1024]{2,1,0:T(8,128)(2,1)S(1)} %bitcast.149), channel_id=1, source_target_pairs={{0,16},{16,0},{32,48},{48,32},{64,80},{80,64},{96,112},{112,96},{1... | collective-permute-start | bytes 1572872 | tf_op jit(solution)/shard_map/ppermute | solution.py:15
  37.5 2.2 %copy-start.3 = (bf16[2,1024,1024]{2,1,0:T(8,128)(2,1)S(1)}, bf16[2,1024,1024]{2,1,0:T(8,128)(2,1)}, u32[]{:S(2)}) copy-start(bf16[2,1024,1024]{2,1,0:T(8,128)(2,1)} %param.6) | copy-start | bytes 12582916
  42.6 43.4 %copy-start.2 = (bf16[32,1024]{1,0:T(8,128)(2,1)S(1)}, bf16[32,1024]{1,0:T(8,128)(2,1)}, u32[]{:S(2)}) copy-start(bf16[32,1024]{1,0:T(8,128)(2,1)} %param.7) | copy-start | bytes 196612
  86.0 33.6 %copy-start.1 = (bf16[32,1024]{1,0:T(8,128)(2,1)}, bf16[32,1024]{1,0:T(8,128)(2,1)S(1)}, u32[]{:S(2)}) copy-start(bf16[32,1024]{1,0:T(8,128)(2,1)S(1)} %subtract_convert_fusion) | copy-start | bytes 196612
  119.7 5.7 %collective-permute-start.10 = (bf16[4,64,1024]{2,1,0:T(8,128)(2,1)S(1)}, bf16[4,64,1024]{2,1,0:T(8,128)(2,1)S(1)}, u32[]{:S(2)}, u32[]{:S(2)}) collective-permute-start(bf16[4,64,1024]{2,1,0:T(8,128)(2,1)S(1)} %fusion.18), channel_id=1, source_target_pairs={{0,16},{16,0},{32,48},{48,32},{64,80},{80,64},{96,112},{112,96},{1... | collective-permute-start | bytes 1572872 | tf_op jit(solution)/shard_map/ppermute | solution.py:15
  123.0 4.9 %collective-permute-start.7 = (bf16[4,64,1024]{2,1,0:T(8,128)(2,1)S(1)}, bf16[4,64,1024]{2,1,0:T(8,128)(2,1)S(1)}, u32[]{:S(2)}, u32[]{:S(2)}) collective-permute-start(bf16[4,64,1024]{2,1,0:T(8,128)(2,1)S(1)} %fusion.17), channel_id=1, source_target_pairs={{0,16},{16,0},{32,48},{48,32},{64,80},{80,64},{96,112},{112,96},{1... | collective-permute-start | bytes 1572872 | tf_op jit(solution)/shard_map/ppermute | solution.py:15
  125.8 11.1 %collective-permute-start.11 = (bf16[2,64,1024]{2,1,0:T(8,128)(2,1)S(1)}, bf16[2,64,1024]{2,1,0:T(8,128)(2,1)S(1)}, u32[]{:S(2)}, u32[]{:S(2)}) collective-permute-start(bf16[2,64,1024]{2,1,0:T(8,128)(2,1)S(1)} %fusion.20), channel_id=1, source_target_pairs={{0,32},{16,48},{32,0},{48,16},{64,96},{80,112},{96,64},{112,80},{1... | collective-permute-start | bytes 786440 | tf_op jit(solution)/shard_map/ppermute | solution.py:32
  128.2 14.7 %collective-permute-start.8 = (bf16[2,64,1024]{2,1,0:T(8,128)(2,1)S(1)}, bf16[2,64,1024]{2,1,0:T(8,128)(2,1)S(1)}, u32[]{:S(2)}, u32[]{:S(2)}) collective-permute-start(bf16[2,64,1024]{2,1,0:T(8,128)(2,1)S(1)} %fusion.19), channel_id=1, source_target_pairs={{0,32},{16,48},{32,0},{48,16},{64,96},{80,112},{96,64},{112,80},{1... | collective-permute-start | bytes 786440 | tf_op jit(solution)/shard_map/ppermute | solution.py:32
  137.0 13.5 %collective-permute-start.12 = (bf16[64,1024]{1,0:T(8,128)(2,1)S(1)}, bf16[64,1024]{1,0:T(8,128)(2,1)S(1)}, u32[]{:S(2)}, u32[]{:S(2)}) collective-permute-start(bf16[64,1024]{1,0:T(8,128)(2,1)S(1)} %fusion.25), channel_id=1, source_target_pairs={{0,64},{16,80},{32,96},{48,112},{64,0},{80,16},{96,32},{112,48},{1... | collective-permute-start | bytes 393224 | tf_op jit(solution)/shard_map/ppermute | solution.py:32
  143.1 11.4 %collective-permute-start.9 = (bf16[64,1024]{1,0:T(8,128)(2,1)S(1)}, bf16[64,1024]{1,0:T(8,128)(2,1)S(1)}, u32[]{:S(2)}, u32[]{:S(2)}) collective-permute-start(bf16[64,1024]{1,0:T(8,128)(2,1)S(1)} %fusion.24), channel_id=1, source_target_pairs={{0,64},{16,80},{32,96},{48,112},{64,0},{80,16},{96,32},{112,48},{1... | collective-permute-start | bytes 393224 | tf_op jit(solution)/shard_map/ppermute | solution.py:32
  150.5 8.1 %collective-permute-start.13 = (bf16[64,1024]{1,0:T(8,128)(2,1)S(1)}, bf16[64,1024]{1,0:T(8,128)(2,1)S(1)}, u32[]{:S(2)}, u32[]{:S(2)}) collective-permute-start(bf16[64,1024]{1,0:T(8,128)(2,1)S(1)} %fusion.21), channel_id=1, source_target_pairs={{128,96},{144,112},{160,64},{176,80},{192,32},{208,48},{224,0},{24... | collective-permute-start | bytes 393224 | tf_op jit(solution)/shard_map/ppermute | solution.py:27
where the time goes:
time: 160 us; the launch traced here: 159 us
  blocking collectives  75.4 us (47%)
  starting transfers between devices  43 us (27%)
  waiting for transfers between devices  27.6 us (17%)
  matrix products  5.11 us (3%)
  other arithmetic  3.91 us (2%)
  local copies, waits for them, and re-layouts  3.16 us (2%)
    all_to_all x2, blocking collectives, over_feat(): return lax.all_to_all(value, 'feat', 0, 0, tiled=True)  75.4 us
    ppermute x8, starting transfers between devices, to_chip(): lax.ppermute(value, 'layer', [(source, source ^ turn * CORES) for source...  25.6 us
    ppermute x8, waiting for transfers between devices, to_chip(): lax.ppermute(value, 'layer', [(source, source ^ turn * CORES) for source...  21.8 us
    ppermute x2, starting transfers between devices, mirrored(): return lax.ppermute(value, 'layer', pairs)  9.3 us
    ppermute x4, starting transfers between devices, swap_cores(): lax.ppermute(value, 'layer', [(source, source ^ 1) for source in range(co...  8.17 us
    ppermute x2, waiting for transfers between devices, mirrored(): return lax.ppermute(value, 'layer', pairs)  5.78 us
  transfers between devices with their start and end apart: 14, of which 9 were waited for; matrix products, arithmetic and copies ran while one was open for 3% of the time, Pallas kernels for 0%

commit v1 on v0

--- a/solution.py
+++ b/solution.py
@@ -15,7 +15,7 @@
     return lax.ppermute(value, "layer", [(source, source ^ 1) for source in range(count)])
 
 
-def mirrored(value, groups, steps):
+def mirrored(value, groups, steps, turn=0):
     count = lax.axis_size("layer")
     chips = groups // CORES
     pairs = []
@@ -23,7 +23,7 @@
         start = source // groups * groups + steps
         chip, core = source % groups // CORES, source % CORES
         if 0 <= start < count:
-            pairs.append((source, start + (chips - 1 - chip) * CORES + core))
+            pairs.append((source, start + (chips - 1 - chip ^ turn) * CORES + core))
     return lax.ppermute(value, "layer", pairs)
 
 
@@ -77,16 +77,17 @@
     tile_mask = jnp.repeat(jnp.repeat(hit, TROWS, axis=0), BLOCK, axis=1)
     own_tile = jnp.where(tile_mask, latents, jnp.zeros_like(latents))
     prior_tile = mirrored(own_tile, groups, groups)
+    prior_far = mirrored(own_tile, groups, groups, 2)
 
-    def spread_over_chips(piece, high, low):
-        far = to_chip(piece, 2)
+    def spread_over_chips(piece, far, high, low):
         pair = ordered(high, piece, far, 0)
         near = to_chip(pair, 1)
         return ordered(low, pair, near, 1).reshape(chips, rows_here, feat_cols)
 
-    own_mine = spread_over_chips(own_tile, upper_pair, upper_chip)
+    own_far = to_chip(own_tile, 2)
+    own_mine = spread_over_chips(own_tile, own_far, upper_pair, upper_chip)
     prior_mine = spread_over_chips(
-        prior_tile, jnp.logical_not(upper_pair), jnp.logical_not(upper_chip)
+        prior_tile, prior_far, jnp.logical_not(upper_pair), jnp.logical_not(upper_chip)
     )
     own_theirs = swap_cores(own_mine)
     prior_theirs = swap_cores(prior_mine)
@@ -115,21 +116,19 @@
         kept, sent = halves(upper_core, terms, 1)
         return kept + swap_cores(sent.astype(jnp.bfloat16)).astype(jnp.float32)
 
-    def summed_over_chips(total, high, low):
+    def near_summed(total, low):
         total = total.reshape(2, chips // 2, rows_here, feat_cols)
         kept, sent = halves(low, total, 1)
         near = to_chip(sent.astype(jnp.bfloat16), 1)
-        total = kept + near.astype(jnp.float32)
-        kept, sent = halves(high, total, 0)
-        far = to_chip(sent.astype(jnp.bfloat16), 2)
-        return kept + far.astype(jnp.float32)
+        return kept + near.astype(jnp.float32)
 
-    to_prior = summed_over_chips(
-        paired(decoders[1]), jnp.logical_not(upper_pair), jnp.logical_not(upper_chip)
-    )
-    from_next = mirrored(to_prior.astype(jnp.bfloat16), groups, -groups)
-    from_next = from_next.astype(jnp.float32)
-    combined = summed_over_chips(paired(decoders[0]), upper_pair, upper_chip) + from_next
+    to_prior = near_summed(paired(decoders[1]), jnp.logical_not(upper_chip))
+    to_prior = halves(jnp.logical_not(upper_pair), to_prior.astype(jnp.bfloat16), 0)
+    from_next = [mirrored(to_prior[0], groups, -groups), mirrored(to_prior[1], groups, -groups, 2)]
+    kept, sent = halves(upper_pair, near_summed(paired(decoders[0]), upper_chip), 0)
+    far = to_chip(sent.astype(jnp.bfloat16), 2)
+    combined = kept + far.astype(jnp.float32)
+    combined = combined + from_next[0].astype(jnp.float32) + from_next[1].astype(jnp.float32)
     latent_grad = jnp.where(tile_mask, combined, jnp.zeros_like(combined))
     return (errors, latent_grad)
 

time: 160 us -> 164 us (1.025)
  starting transfers between devices: 43 us -> 47 us
    ppermute x8 -> x6, waiting for transfers between devices: 21.8 us -> 12.2 us  [to_chip(): lax.ppermute(value, 'layer', [(source, source ^ turn * CORES) for source...]
    ppermute x2 -> x4, waiting for transfers between devices: 5.78 us -> 14.4 us  [mirrored(): return lax.ppermute(value, 'layer', pairs)]
    ppermute x2 -> x4, starting transfers between devices: 9.3 us -> 16.6 us  [mirrored(): return lax.ppermute(value, 'layer', pairs)]
    ppermute x8 -> x6, starting transfers between devices: 25.6 us -> 22.3 us  [to_chip(): lax.ppermute(value, 'layer', [(source, source ^ turn * CORES) for source...]
  transfers between devices with their start and end apart: 14 -> 14, of which waited for: 9 -> 8; matrix products, arithmetic and copies ran while one was open for 3% -> 2% of each run, Pallas kernels for 0% -> 0%
where the time goes in v1:
time: 164 us
  blocking collectives  75.2 us (46%)
  starting transfers between devices  47 us (29%)
  waiting for transfers between devices  28.2 us (17%)
  matrix products  5.11 us (3%)
  other arithmetic  3.89 us (2%)
  local copies, waits for them, and re-layouts  3.16 us (2%)
    all_to_all x2, blocking collectives, over_feat(): return lax.all_to_all(value, 'feat', 0, 0, tiled=True)  75.2 us
    ppermute x6, starting transfers between devices, to_chip(): lax.ppermute(value, 'layer', [(source, source ^ turn * CORES) for source...  22.3 us
    ppermute x4, starting transfers between devices, mirrored(): return lax.ppermute(value, 'layer', pairs)  16.6 us
    ppermute x4, waiting for transfers between devices, mirrored(): return lax.ppermute(value, 'layer', pairs)  14.4 us
    ppermute x6, waiting for transfers between devices, to_chip(): lax.ppermute(value, 'layer', [(source, source ^ turn * CORES) for source...  12.2 us
    ppermute x4, starting transfers between devices, swap_cores(): lax.ppermute(value, 'layer', [(source, source ^ 1) for source in range(co...  8.17 us
  transfers between devices with their start and end apart: 14, of which 8 were waited for; matrix products, arithmetic and copies ran while one was open for 2% of the time, Pallas kernels for 0%

profile of v1, /device:TPU:2, one launch (start us, length us, event | category | flops | bytes accessed | tf_op | source)
XLA Modules:
  0.0 163.7 jit_solution(1683220245105639883)
XLA Ops:
  0.7 0.7 copy-done
  1.7 0.9 bitcast_select_fusion.1
  2.7 5.4 %collective-permute-start.1 = (bf16[64,1024]{1,0:T(8,128)(2,1)S(1)}, bf16[64,1024]{1,0:T(8,128)(2,1)S(1)}, u32[]{:S(2)}, u32[]{:S(2)}) collective-permute-start(bf16[64,1024]{1,0:T(8,128)(2,1)S(1)} %bitcast_select_fusion.1), channel_id=1, source_target_pairs={{0,224},{16,240},{32,192},{48,208},{64,160},{80,176},{96,128},{112... | collective-permute-start | bytes 393224 | tf_op jit(solution)/shard_map/ppermute | solution.py:27
  8.1 2.9 %collective-permute-start = (bf16[64,1024]{1,0:T(8,128)(2,1)S(1)}, bf16[64,1024]{1,0:T(8,128)(2,1)S(1)}, u32[]{:S(2)}, u32[]{:S(2)}) collective-permute-start(bf16[64,1024]{1,0:T(8,128)(2,1)S(1)} %bitcast_select_fusion.1), channel_id=1, source_target_pairs={{0,160},{16,176},{32,128},{48,144},{64,224},{80,240},{96,192},{112... | collective-permute-start | bytes 393224 | tf_op jit(solution)/shard_map/ppermute | solution.py:27
  10.9 4.0 %collective-permute-start.4 = (bf16[64,1024]{1,0:T(8,128)(2,1)S(1)}, bf16[64,1024]{1,0:T(8,128)(2,1)S(1)}, u32[]{:S(2)}, u32[]{:S(2)}) collective-permute-start(bf16[64,1024]{1,0:T(8,128)(2,1)S(1)} %bitcast_select_fusion.1), channel_id=1, source_target_pairs={{0,64},{16,80},{32,96},{48,112},{64,0},{80,16},{96,32},{112,48},{1... | collective-permute-start | bytes 393224 | tf_op jit(solution)/shard_map/ppermute | solution.py:32
  15.0 2.4 %collective-permute-done.1 = bf16[64,1024]{1,0:T(8,128)(2,1)S(1)} collective-permute-done((bf16[64,1024]{1,0:T(8,128)(2,1)S(1)}, bf16[64,1024]{1,0:T(8,128)(2,1)S(1)}, u32[]{:S(2)}, u32[]{:S(2)}) %collective-permute-start.1) | collective-permute-done | bytes 131104 | tf_op jit(solution)/shard_map/ppermute | solution.py:27
  17.4 1.8 %collective-permute-done = bf16[64,1024]{1,0:T(8,128)(2,1)S(1)} collective-permute-done((bf16[64,1024]{1,0:T(8,128)(2,1)S(1)}, bf16[64,1024]{1,0:T(8,128)(2,1)S(1)}, u32[]{:S(2)}, u32[]{:S(2)}) %collective-permute-start) | collective-permute-done | bytes 131104 | tf_op jit(solution)/shard_map/ppermute | solution.py:27
  19.3 6.7 %collective-permute-start.2 = (bf16[2,64,1024]{2,1,0:T(8,128)(2,1)S(1)}, bf16[2,64,1024]{2,1,0:T(8,128)(2,1)S(1)}, u32[]{:S(2)}, u32[]{:S(2)}) collective-permute-start(bf16[2,64,1024]{2,1,0:T(8,128)(2,1)S(1)} %pad_maximum_fusion.4), channel_id=1, source_target_pairs={{0,32},{16,48},{32,0},{48,16},{64,96},{80,112},{96,64},{112,80},{1... | collective-permute-start | bytes 786440 | tf_op jit(solution)/shard_map/ppermute | solution.py:32
  26.1 1.9 %collective-permute-start.5 = (bf16[2,64,1024]{2,1,0:T(8,128)(2,1)S(1)}, bf16[2,64,1024]{2,1,0:T(8,128)(2,1)S(1)}, u32[]{:S(2)}, u32[]{:S(2)}) collective-permute-start(bf16[2,64,1024]{2,1,0:T(8,128)(2,1)S(1)} %pad_maximum_fusion.5), channel_id=1, source_target_pairs={{0,32},{16,48},{32,0},{48,16},{64,96},{80,112},{96,64},{112,80},{1... | collective-permute-start | bytes 786440 | tf_op jit(solution)/shard_map/ppermute | solution.py:32
  28.0 5.1 %collective-permute-done.2 = bf16[2,64,1024]{2,1,0:T(8,128)(2,1)S(1)} collective-permute-done((bf16[2,64,1024]{2,1,0:T(8,128)(2,1)S(1)}, bf16[2,64,1024]{2,1,0:T(8,128)(2,1)S(1)}, u32[]{:S(2)}, u32[]{:S(2)}) %collective-permute-start.2) | collective-permute-done | bytes 262176 | tf_op jit(solution)/shard_map/ppermute | solution.py:32
  33.3 1.9 %collective-permute-start.3 = (bf16[4,64,1024]{2,1,0:T(8,128)(2,1)S(1)}, bf16[4,64,1024]{2,1,0:T(8,128)(2,1)S(1)}, u32[]{:S(2)}, u32[]{:S(2)}) collective-permute-start(bf16[4,64,1024]{2,1,0:T(8,128)(2,1)S(1)} %bitcast.150), channel_id=1, source_target_pairs={{0,16},{16,0},{32,48},{48,32},{64,80},{80,64},{96,112},{112,96},{1... | collective-permute-start | bytes 1572872 | tf_op jit(solution)/shard_map/ppermute | solution.py:15
  35.2 2.2 %collective-permute-done.5 = bf16[2,64,1024]{2,1,0:T(8,128)(2,1)S(1)} collective-permute-done((bf16[2,64,1024]{2,1,0:T(8,128)(2,1)S(1)}, bf16[2,64,1024]{2,1,0:T(8,128)(2,1)S(1)}, u32[]{:S(2)}, u32[]{:S(2)}) %collective-permute-start.5) | collective-permute-done | bytes 262176 | tf_op jit(solution)/shard_map/ppermute | solution.py:32
  37.6 1.9 %collective-permute-start.6 = (bf16[4,64,1024]{2,1,0:T(8,128)(2,1)S(1)}, bf16[4,64,1024]{2,1,0:T(8,128)(2,1)S(1)}, u32[]{:S(2)}, u32[]{:S(2)}) collective-permute-start(bf16[4,64,1024]{2,1,0:T(8,128)(2,1)S(1)} %bitcast.151), channel_id=1, source_target_pairs={{0,16},{16,0},{32,48},{48,32},{64,80},{80,64},{96,112},{112,96},{1... | collective-permute-start | bytes 1572872 | tf_op jit(solution)/shard_map/ppermute | solution.py:15
  39.8 1.6 collective-permute-done.6
  41.7 2.0 %copy-done.3 = bf16[2,1024,1024]{2,1,0:T(8,128)(2,1)S(1)} copy-done((bf16[2,1024,1024]{2,1,0:T(8,128)(2,1)S(1)}, bf16[2,1024,1024]{2,1,0:T(8,128)(2,1)}, u32[]{:S(2)}) %copy-start.3) | copy-done | bytes 4194328
  43.7 1.3 fusion.4
  44.9 1.3 add_convert_fusion
  46.2 42.6 %all_to_all.10 = bf16[16,32,1024]{2,1,0:T(8,128)(2,1)S(1)} all-to-all(bf16[16,32,1024]{2,1,0:T(8,128)(2,1)S(1)} %bitcast.155), channel_id=1, replica_groups=mesh['layer'=32,'feat'=16] {'feat'}, dimensions={0} | all-to-all | bytes 2097152 | tf_op jit(solution)/shard_map/all_to_all | solution.py:50
  89.2 32.6 %all_to_all.11 = bf16[16,32,1024]{2,1,0:T(8,128)(2,1)S(1)} all-to-all(bf16[16,32,1024]{2,1,0:T(8,128)(2,1)S(1)} %broadcast_in_dim.22), channel_id=1, replica_groups=mesh['layer'=32,'feat'=16] {'feat'}, dimensions={0} | all-to-all | bytes 2097152 | tf_op jit(solution)/shard_map/all_to_all | solution.py:50
  121.8 1.3 fusion
  123.2 1.9 %collective-permute-start.10 = (bf16[4,64,1024]{2,1,0:T(8,128)(2,1)S(1)}, bf16[4,64,1024]{2,1,0:T(8,128)(2,1)S(1)}, u32[]{:S(2)}, u32[]{:S(2)}) collective-permute-start(bf16[4,64,1024]{2,1,0:T(8,128)(2,1)S(1)} %fusion.18), channel_id=1, source_target_pairs={{0,16},{16,0},{32,48},{48,32},{64,80},{80,64},{96,112},{112,96},{1... | collective-permute-start | bytes 1572872 | tf_op jit(solution)/shard_map/ppermute | solution.py:15
  125.1 1.3 fusion.2
  126.5 2.4 %collective-permute-start.7 = (bf16[4,64,1024]{2,1,0:T(8,128)(2,1)S(1)}, bf16[4,64,1024]{2,1,0:T(8,128)(2,1)S(1)}, u32[]{:S(2)}, u32[]{:S(2)}) collective-permute-start(bf16[4,64,1024]{2,1,0:T(8,128)(2,1)S(1)} %fusion.17), channel_id=1, source_target_pairs={{0,16},{16,0},{32,48},{48,32},{64,80},{80,64},{96,112},{112,96},{1... | collective-permute-start | bytes 1572872 | tf_op jit(solution)/shard_map/ppermute | solution.py:15
  129.3 3.6 %collective-permute-start.11 = (bf16[2,64,1024]{2,1,0:T(8,128)(2,1)S(1)}, bf16[2,64,1024]{2,1,0:T(8,128)(2,1)S(1)}, u32[]{:S(2)}, u32[]{:S(2)}) collective-permute-start(bf16[2,64,1024]{2,1,0:T(8,128)(2,1)S(1)} %fusion.21), channel_id=1, source_target_pairs={{0,32},{16,48},{32,0},{48,16},{64,96},{80,112},{96,64},{112,80},{1... | collective-permute-start | bytes 786440 | tf_op jit(solution)/shard_map/ppermute | solution.py:32
  133.3 2.2 %collective-permute-start.8 = (bf16[2,64,1024]{2,1,0:T(8,128)(2,1)S(1)}, bf16[2,64,1024]{2,1,0:T(8,128)(2,1)S(1)}, u32[]{:S(2)}, u32[]{:S(2)}) collective-permute-start(bf16[2,64,1024]{2,1,0:T(8,128)(2,1)S(1)} %fusion.20), channel_id=1, source_target_pairs={{0,32},{16,48},{32,0},{48,16},{64,96},{80,112},{96,64},{112,80},{1... | collective-permute-start | bytes 786440 | tf_op jit(solution)/shard_map/ppermute | solution.py:32
  135.5 4.9 %collective-permute-done.11 = bf16[2,64,1024]{2,1,0:T(8,128)(2,1)S(1)} collective-permute-done((bf16[2,64,1024]{2,1,0:T(8,128)(2,1)S(1)}, bf16[2,64,1024]{2,1,0:T(8,128)(2,1)S(1)}, u32[]{:S(2)}, u32[]{:S(2)}) %collective-permute-start.11) | collective-permute-done | bytes 262176 | tf_op jit(solution)/shard_map/ppermute | solution.py:32
  140.5 5.9 %collective-permute-start.12 = (bf16[64,1024]{1,0:T(8,128)(2,1)S(1)}, bf16[64,1024]{1,0:T(8,128)(2,1)S(1)}, u32[]{:S(2)}, u32[]{:S(2)}) collective-permute-start(bf16[64,1024]{1,0:T(8,128)(2,1)S(1)} %get-tuple-element.10), channel_id=1, source_target_pairs={{128,96},{144,112},{160,64},{176,80},{192,32},{208,48},{224,0},{24... | collective-permute-start | bytes 393224 | tf_op jit(solution)/shard_map/ppermute | solution.py:27
  146.4 2.4 %collective-permute-start.13 = (bf16[64,1024]{1,0:T(8,128)(2,1)S(1)}, bf16[64,1024]{1,0:T(8,128)(2,1)S(1)}, u32[]{:S(2)}, u32[]{:S(2)}) collective-permute-start(bf16[64,1024]{1,0:T(8,128)(2,1)S(1)} %get-tuple-element.11), channel_id=1, source_target_pairs={{128,32},{144,48},{160,0},{176,16},{192,96},{208,112},{224,64},{24... | collective-permute-start | bytes 393224 | tf_op jit(solution)/shard_map/ppermute | solution.py:27
  149.0 3.8 %collective-permute-start.9 = (bf16[64,1024]{1,0:T(8,128)(2,1)S(1)}, bf16[64,1024]{1,0:T(8,128)(2,1)S(1)}, u32[]{:S(2)}, u32[]{:S(2)}) collective-permute-start(bf16[64,1024]{1,0:T(8,128)(2,1)S(1)} %fusion.25), channel_id=1, source_target_pairs={{0,64},{16,80},{32,96},{48,112},{64,0},{80,16},{96,32},{112,48},{1... | collective-permute-start | bytes 393224 | tf_op jit(solution)/shard_map/ppermute | solution.py:32
  152.7 0.8 collective-permute-done.12
  153.5 9.4 %collective-permute-done.13 = bf16[64,1024]{1,0:T(8,128)(2,1)S(1)} collective-permute-done((bf16[64,1024]{1,0:T(8,128)(2,1)S(1)}, bf16[64,1024]{1,0:T(8,128)(2,1)S(1)}, u32[]{:S(2)}, u32[]{:S(2)}) %collective-permute-start.13) | collective-permute-done | bytes 131104 | tf_op jit(solution)/shard_map/ppermute | solution.py:27
  162.9 0.8 fusion.24
  (45 shorter events, 2.7 us)
Async XLA Ops:
  0.6 0.8 copy-start
  2.7 14.8 %collective-permute-start.1 = (bf16[64,1024]{1,0:T(8,128)(2,1)S(1)}, bf16[64,1024]{1,0:T(8,128)(2,1)S(1)}, u32[]{:S(2)}, u32[]{:S(2)}) collective-permute-start(bf16[64,1024]{1,0:T(8,128)(2,1)S(1)} %bitcast_select_fusion.1), channel_id=1, source_target_pairs={{0,224},{16,240},{32,192},{48,208},{64,160},{80,176},{96,128},{112... | collective-permute-start | bytes 393224 | tf_op jit(solution)/shard_map/ppermute | solution.py:27
  8.1 11.2 %collective-permute-start = (bf16[64,1024]{1,0:T(8,128)(2,1)S(1)}, bf16[64,1024]{1,0:T(8,128)(2,1)S(1)}, u32[]{:S(2)}, u32[]{:S(2)}) collective-permute-start(bf16[64,1024]{1,0:T(8,128)(2,1)S(1)} %bitcast_select_fusion.1), channel_id=1, source_target_pairs={{0,160},{16,176},{32,128},{48,144},{64,224},{80,240},{96,192},{112... | collective-permute-start | bytes 393224 | tf_op jit(solution)/shard_map/ppermute | solution.py:27
  10.9 15.1 %collective-permute-start.4 = (bf16[64,1024]{1,0:T(8,128)(2,1)S(1)}, bf16[64,1024]{1,0:T(8,128)(2,1)S(1)}, u32[]{:S(2)}, u32[]{:S(2)}) collective-permute-start(bf16[64,1024]{1,0:T(8,128)(2,1)S(1)} %bitcast_select_fusion.1), channel_id=1, source_target_pairs={{0,64},{16,80},{32,96},{48,112},{64,0},{80,16},{96,32},{112,48},{1... | collective-permute-start | bytes 393224 | tf_op jit(solution)/shard_map/ppermute | solution.py:32
  19.3 13.9 %collective-permute-start.2 = (bf16[2,64,1024]{2,1,0:T(8,128)(2,1)S(1)}, bf16[2,64,1024]{2,1,0:T(8,128)(2,1)S(1)}, u32[]{:S(2)}, u32[]{:S(2)}) collective-permute-start(bf16[2,64,1024]{2,1,0:T(8,128)(2,1)S(1)} %pad_maximum_fusion.4), channel_id=1, source_target_pairs={{0,32},{16,48},{32,0},{48,16},{64,96},{80,112},{96,64},{112,80},{1... | collective-permute-start | bytes 786440 | tf_op jit(solution)/shard_map/ppermute | solution.py:32
  26.1 11.3 %collective-permute-start.5 = (bf16[2,64,1024]{2,1,0:T(8,128)(2,1)S(1)}, bf16[2,64,1024]{2,1,0:T(8,128)(2,1)S(1)}, u32[]{:S(2)}, u32[]{:S(2)}) collective-permute-start(bf16[2,64,1024]{2,1,0:T(8,128)(2,1)S(1)} %pad_maximum_fusion.5), channel_id=1, source_target_pairs={{0,32},{16,48},{32,0},{48,16},{64,96},{80,112},{96,64},{112,80},{1... | collective-permute-start | bytes 786440 | tf_op jit(solution)/shard_map/ppermute | solution.py:32
  33.3 6.2 %collective-permute-start.3 = (bf16[4,64,1024]{2,1,0:T(8,128)(2,1)S(1)}, bf16[4,64,1024]{2,1,0:T(8,128)(2,1)S(1)}, u32[]{:S(2)}, u32[]{:S(2)}) collective-permute-start(bf16[4,64,1024]{2,1,0:T(8,128)(2,1)S(1)} %bitcast.150), channel_id=1, source_target_pairs={{0,16},{16,0},{32,48},{48,32},{64,80},{80,64},{96,112},{112,96},{1... | collective-permute-start | bytes 1572872 | tf_op jit(solution)/shard_map/ppermute | solution.py:15
  37.6 3.8 %collective-permute-start.6 = (bf16[4,64,1024]{2,1,0:T(8,128)(2,1)S(1)}, bf16[4,64,1024]{2,1,0:T(8,128)(2,1)S(1)}, u32[]{:S(2)}, u32[]{:S(2)}) collective-permute-start(bf16[4,64,1024]{2,1,0:T(8,128)(2,1)S(1)} %bitcast.151), channel_id=1, source_target_pairs={{0,16},{16,0},{32,48},{48,32},{64,80},{80,64},{96,112},{112,96},{1... | collective-permute-start | bytes 1572872 | tf_op jit(solution)/shard_map/ppermute | solution.py:15
  41.5 2.2 %copy-start.3 = (bf16[2,1024,1024]{2,1,0:T(8,128)(2,1)S(1)}, bf16[2,1024,1024]{2,1,0:T(8,128)(2,1)}, u32[]{:S(2)}) copy-start(bf16[2,1024,1024]{2,1,0:T(8,128)(2,1)} %param.6) | copy-start | bytes 12582916
  46.2 42.8 %copy-start.2 = (bf16[32,1024]{1,0:T(8,128)(2,1)S(1)}, bf16[32,1024]{1,0:T(8,128)(2,1)}, u32[]{:S(2)}) copy-start(bf16[32,1024]{1,0:T(8,128)(2,1)} %param.7) | copy-start | bytes 196612
  89.1 34.0 %copy-start.1 = (bf16[32,1024]{1,0:T(8,128)(2,1)}, bf16[32,1024]{1,0:T(8,128)(2,1)S(1)}, u32[]{:S(2)}) copy-start(bf16[32,1024]{1,0:T(8,128)(2,1)S(1)} %subtract_convert_fusion) | copy-start | bytes 196612
  123.2 5.7 %collective-permute-start.10 = (bf16[4,64,1024]{2,1,0:T(8,128)(2,1)S(1)}, bf16[4,64,1024]{2,1,0:T(8,128)(2,1)S(1)}, u32[]{:S(2)}, u32[]{:S(2)}) collective-permute-start(bf16[4,64,1024]{2,1,0:T(8,128)(2,1)S(1)} %fusion.18), channel_id=1, source_target_pairs={{0,16},{16,0},{32,48},{48,32},{64,80},{80,64},{96,112},{112,96},{1... | collective-permute-start | bytes 1572872 | tf_op jit(solution)/shard_map/ppermute | solution.py:15
  126.5 6.4 %collective-permute-start.7 = (bf16[4,64,1024]{2,1,0:T(8,128)(2,1)S(1)}, bf16[4,64,1024]{2,1,0:T(8,128)(2,1)S(1)}, u32[]{:S(2)}, u32[]{:S(2)}) collective-permute-start(bf16[4,64,1024]{2,1,0:T(8,128)(2,1)S(1)} %fusion.17), channel_id=1, source_target_pairs={{0,16},{16,0},{32,48},{48,32},{64,80},{80,64},{96,112},{112,96},{1... | collective-permute-start | bytes 1572872 | tf_op jit(solution)/shard_map/ppermute | solution.py:15
  129.3 11.1 %collective-permute-start.11 = (bf16[2,64,1024]{2,1,0:T(8,128)(2,1)S(1)}, bf16[2,64,1024]{2,1,0:T(8,128)(2,1)S(1)}, u32[]{:S(2)}, u32[]{:S(2)}) collective-permute-start(bf16[2,64,1024]{2,1,0:T(8,128)(2,1)S(1)} %fusion.21), channel_id=1, source_target_pairs={{0,32},{16,48},{32,0},{48,16},{64,96},{80,112},{96,64},{112,80},{1... | collective-permute-start | bytes 786440 | tf_op jit(solution)/shard_map/ppermute | solution.py:32
  133.3 15.5 %collective-permute-start.8 = (bf16[2,64,1024]{2,1,0:T(8,128)(2,1)S(1)}, bf16[2,64,1024]{2,1,0:T(8,128)(2,1)S(1)}, u32[]{:S(2)}, u32[]{:S(2)}) collective-permute-start(bf16[2,64,1024]{2,1,0:T(8,128)(2,1)S(1)} %fusion.20), channel_id=1, source_target_pairs={{0,32},{16,48},{32,0},{48,16},{64,96},{80,112},{96,64},{112,80},{1... | collective-permute-start | bytes 786440 | tf_op jit(solution)/shard_map/ppermute | solution.py:32
  140.5 13.0 %collective-permute-start.12 = (bf16[64,1024]{1,0:T(8,128)(2,1)S(1)}, bf16[64,1024]{1,0:T(8,128)(2,1)S(1)}, u32[]{:S(2)}, u32[]{:S(2)}) collective-permute-start(bf16[64,1024]{1,0:T(8,128)(2,1)S(1)} %get-tuple-element.10), channel_id=1, source_target_pairs={{128,96},{144,112},{160,64},{176,80},{192,32},{208,48},{224,0},{24... | collective-permute-start | bytes 393224 | tf_op jit(solution)/shard_map/ppermute | solution.py:27
  146.4 16.5 %collective-permute-start.13 = (bf16[64,1024]{1,0:T(8,128)(2,1)S(1)}, bf16[64,1024]{1,0:T(8,128)(2,1)S(1)}, u32[]{:S(2)}, u32[]{:S(2)}) collective-permute-start(bf16[64,1024]{1,0:T(8,128)(2,1)S(1)} %get-tuple-element.11), channel_id=1, source_target_pairs={{128,32},{144,48},{160,0},{176,16},{192,96},{208,112},{224,64},{24... | collective-permute-start | bytes 393224 | tf_op jit(solution)/shard_map/ppermute | solution.py:27
  149.0 13.9 %collective-permute-start.9 = (bf16[64,1024]{1,0:T(8,128)(2,1)S(1)}, bf16[64,1024]{1,0:T(8,128)(2,1)S(1)}, u32[]{:S(2)}, u32[]{:S(2)}) collective-permute-start(bf16[64,1024]{1,0:T(8,128)(2,1)S(1)} %fusion.25), channel_id=1, source_target_pairs={{0,64},{16,80},{32,96},{48,112},{64,0},{80,16},{96,32},{112,48},{1... | collective-permute-start | bytes 393224 | tf_op jit(solution)/shard_map/ppermute | solution.py:32
